TPU v7x, 32 devices: a whole 2x2x4 slice. The times are simulated.
32 devices in a mesh: groups: 2 (over x), hist: 8 (over z, y), cand: 2 (over core).
Axes of the slice: x: 2, y: 2, z: 4, core: 2. Of those that a mesh axis runs over, the one named last changes fastest.
Arguments:
- candidates: bfloat16 [16, 1024, 512], P(('groups', 'hist'), 'cand'), parts along dimension 0, may hold values from -6 to 6
- hist_keys: bfloat16 [16, 1024, 512], P('groups', ('hist', 'cand')), parts along dimension 0, may hold values from -10 to 10
- hist_values: bfloat16 [16, 1024, 512], P('groups', ('hist', 'cand')), parts along dimension 0, may hold values from -6 to 6
- block_mask: int32 [16, 8, 8], P(('groups', 'hist')), parts along dimension 0, may hold values 0 or 1
- hist_blocks: int32 [16], P(('groups', 'hist')), parts along dimension 0, may hold values from 1 to 8, as said below
- proj_weight: bfloat16 [512, 1024], replicated, may hold values from -0.25 to 0.25
- out_weight: bfloat16 [512, 512], replicated, may hold values from -0.25 to 0.25
Outputs:
- cand_out: bfloat16 [16, 1024, 512], P(('groups', 'hist'), 'cand'), parts along dimension 0
There are 2 independent parts, one for each index of `groups`. A program takes and returns all parts, laid end to end along the dimension named above; an argument that names none is the same for every part. Nothing has to cross between parts.
Inputs may be any that keep to these rules, and one draw needn't show every extreme that they name: `hist_blocks`: some user has all 8 blocks.
All inputs are finite; a program needn't handle non-finite values. No bound on the sum of `block_mask` on one device may be relied on, other than what follows from the above.
Results may differ from a plain program's by a relative error of at most 0.013.
Values may be sent and summed in bfloat16 or wider, within the bound.
A program may use at most 64 MiB of HBM per device.

v0:
```python
import jax
import jax.numpy as jnp
from jax import lax
from jax.sharding import PartitionSpec as P

HEADS = 8
BLK = 128
EPS = 1e-05


def layer_norm(values_in):
    center = values_in - jnp.mean(values_in, axis=-1, keepdims=True)
    spread = jnp.mean(center * center, axis=-1, keepdims=True)
    return center * lax.rsqrt(spread + EPS)


def attend(running, query_heads, mask_rows, key_piece, value_piece, slab_count, group_rows, stride):
    piece_width = key_piece.shape[1]
    query_count = query_heads.shape[0]
    head_count = query_heads.shape[1]
    head_size = query_heads.shape[2]
    block_count = mask_rows.shape[0]
    block_total = mask_rows.shape[1]
    slab_keys = group_rows * piece_width
    score_scale = head_size ** (-0.5)

    def add_slab(slab_index, summed):
        key_slab = lax.dynamic_slice_in_dim(key_piece, slab_index * group_rows, group_rows, 0)
        value_slab = lax.dynamic_slice_in_dim(value_piece, slab_index * group_rows, group_rows, 0)
        key_slab = key_slab.reshape(slab_keys, head_count, head_size)
        value_slab = value_slab.reshape(slab_keys, head_count, head_size)
        positions = (slab_index * group_rows + jnp.arange(group_rows, dtype=jnp.int32))[
            :, None
        ] * stride
        positions = (positions + jnp.arange(piece_width, dtype=jnp.int32)[None, :]).reshape(
            slab_keys
        )
        onehot = (
            positions[None, :] // BLK == jnp.arange(block_total, dtype=jnp.int32)[:, None]
        ).astype(jnp.float32)
        key_mask = jnp.dot(mask_rows, onehot, preferred_element_type=jnp.float32)
        scores = (
            jnp.einsum("qhd,khd->hqk", query_heads, key_slab, preferred_element_type=jnp.float32)
            * score_scale
        )
        gated_scores = (
            jax.nn.silu(scores).reshape(head_count, block_count, BLK, slab_keys)
            * key_mask[None, :, None, :]
        )
        weights = gated_scores.reshape(head_count, query_count, slab_keys).astype(jnp.bfloat16)
        return summed + jnp.einsum(
            "hqk,khd->qhd", weights, value_slab, preferred_element_type=jnp.float32
        )

    return lax.fori_loop(0, slab_count, add_slab, running)


def on_device(candidates, hist_keys, hist_values, block_mask, hist_blocks, proj_weight, out_weight):
    cand_rows = candidates[0]
    own_count = cand_rows.shape[0]
    width_model = cand_rows.shape[1]
    head_count = HEADS
    head_size = width_model // head_count
    normed = layer_norm(cand_rows.astype(jnp.float32)).astype(jnp.bfloat16)
    projected = jax.nn.silu(
        jnp.dot(normed, proj_weight, preferred_element_type=jnp.float32)
    ).astype(jnp.bfloat16)
    gate_rows = projected[:, :width_model]
    queries = projected[:, width_model:]
    query_heads = queries.reshape(own_count, head_count, head_size)
    block_total = block_mask.shape[2]
    live_blocks = (jnp.arange(block_total, dtype=jnp.int32) < hist_blocks[0]).astype(jnp.float32)
    mask_eff = block_mask[0].astype(jnp.float32) * live_blocks[None, :]
    arrived_keys, arrived_values = (
        lax.all_to_all(hist_keys[:, None], "hist", split_axis=0, concat_axis=1, tiled=True),
        lax.all_to_all(hist_values[:, None], "hist", split_axis=0, concat_axis=1, tiled=True),
    )
    key_rows = arrived_keys[0]
    value_rows = arrived_values[0]
    hist_count = lax.axis_size("hist")
    cand_count = lax.axis_size("cand")
    cand_index = lax.axis_index("cand")
    per_device = key_rows.shape[1]
    stride = cand_count * per_device
    group_rows = min(8, hist_count)
    slab_count = hist_count // group_rows
    own_blocks = own_count // BLK
    own_mask = lax.dynamic_slice_in_dim(mask_eff, cand_index * own_blocks, own_blocks, 0)
    empty = jnp.zeros((own_count, head_count, head_size), jnp.float32)
    attended = attend(
        empty,
        query_heads,
        own_mask,
        lax.all_gather(key_rows, "cand", axis=1, tiled=True),
        lax.all_gather(value_rows, "cand", axis=1, tiled=True),
        slab_count,
        group_rows,
        stride,
    )
    attended = attended.reshape(own_count, width_model)
    mixed = (layer_norm(attended) * gate_rows.astype(jnp.float32)).astype(jnp.bfloat16)
    result = cand_rows.astype(jnp.float32) + jnp.dot(
        mixed, out_weight, preferred_element_type=jnp.float32
    )
    return result.astype(jnp.bfloat16)[None]


def solution(mesh):
    in_specs = (
        P(("groups", "hist"), "cand", None),
        P("groups", ("hist", "cand"), None),
        P("groups", ("hist", "cand"), None),
        P(("groups", "hist"), None, None),
        P(("groups", "hist")),
        P(),
        P(),
    )
    out_specs = P(("groups", "hist"), "cand", None)
    return jax.shard_map(
        on_device, mesh=mesh, in_specs=in_specs, out_specs=out_specs, check_vma=False
    )
```

profile of v0, /device:TPU:0, one launch (start us, length us, event | category | flops | bytes accessed | tf_op | source)
XLA Modules:
  0.0 81.3 jit_solution(10235428924594484104)
XLA Ops:
  6.5 0.0 copy-start
  6.5 0.0 copy-start.1
  6.5 0.0 all-gather.5.cloned.1.call-start
  6.5 22.1 %all_to_all.8 = bf16[8,1,64,512]{3,2,1,0:T(8,128)(2,1)} all-to-all(bf16[8,1,64,512]{3,2,1,0:T(8,128)(2,1)} %bitcast.74), channel_id=1, replica_groups=mesh['groups'=2,'hist'=8,'cand'=2] {'hist'}, dimensions={0} | all-to-all | bytes 1048576 | tf_op jit(solution)/shard_map/all_to_all | solution.py:75
  28.6 0.0 all-gather.5.cloned.1.call-update
  28.6 3.6 %all-to-all-start.1 = ((bf16[8,1,64,512]{3,2,1,0:T(8,128)(2,1)}), bf16[8,1,64,512]{3,2,1,0:T(8,128)(2,1)S(1)}, u32[]{:S(2)}, u32[]{:S(2)}) async-start(bf16[8,1,64,512]{3,2,1,0:T(8,128)(2,1)} %bitcast.75), calls=%async_computation.1 | async-start | bytes 1048576 | tf_op jit(solution)/shard_map/all_to_all | solution.py:76
  32.2 0.0 all-gather.7.cloned.1.call-start
  32.3 0.0 copy-done.1
  32.3 0.1 convert_reduce_fusion
  32.5 0.3 fusion.6
  32.8 13.6 %all-to-all-done.1 = bf16[8,1,64,512]{3,2,1,0:T(8,128)(2,1)S(1)} async-done(((bf16[8,1,64,512]{3,2,1,0:T(8,128)(2,1)}), bf16[8,1,64,512]{3,2,1,0:T(8,128)(2,1)S(1)}, u32[]{:S(2)}, u32[]{:S(2)}) %all-to-all-start.1) | async-done | bytes 524320 | tf_op jit(solution)/shard_map/all_to_all | solution.py:76
  46.4 0.0 copy-start.2
  46.4 0.8 copy-done.2
  47.2 0.0 all-gather.7.cloned.1.call-update
  47.2 0.0 copy-done
  47.3 1.0 %multiply_convert_fusion.1 = bf16[512,1024]{1,0:T(8,128)(2,1)S(1)} fusion(bf16[512,1024]{1,0:T(8,128)(2,1)S(1)} %copy-done, bf16[1,512,512]{2,1,0:T(8,128)(2,1)S(1)} %copy-done.1, f32[512]{0:T(512)S(1)} %add_rsqrt_fusion.1, f32[512]{0:T(512)S(1)} %broadcast_multiply_fusion.1), kind=kOutput, calls=%fused_computation.1 | convolution fusion | flops 540540928 | bytes 2625536 | tf_op jit(solution)/shard_map/dot_general | solution.py:66
  48.3 0.0 copy-start.3
  48.3 0.0 copy-start.6
  49.1 1.0 %copy.16 = bf16[512,512]{0,1:T(8,128)(2,1)} copy(bf16[512,512]{1,0:T(8,128)(2,1)S(1)} %slice.8) | data formatting | bytes 1048576 | tf_op jit(solution)/shard_map/slice | solution.py:69
  50.1 0.1 add_select_fusion
  50.2 0.0 copy-done.6
  50.2 0.1 fusion.19
  50.3 0.0 copy-done.3
  50.3 0.0 all-gather.5.cloned.1.call-done
  50.3 1.7 %copy.17 = bf16[8,1,128,512]{2,0,3,1:T(8,128)(2,1)S(1)} copy(bf16[8,1,128,512]{3,2,1,0:T(8,128)(2,1)} %all-gather.5.cloned.1.call-done) | data formatting | bytes 2097152 | tf_op jit(solution)/shard_map/all_gather | solution.py:94
  52.0 1.3 %reshape.148 = bf16[1024,8,64]{0,2,1:T(8,128)(2,1)} reshape(bf16[8,1,128,512]{2,0,3,1:T(8,128)(2,1)S(1)} %copy.17) | data formatting | bytes 2097152 | tf_op jit(solution)/shard_map/while/body/eval_jaxpr/reshape | solution.py:30
  53.3 2.2 %all-gather.7.cloned.1.call-done = bf16[8,1,128,512]{3,2,1,0:T(8,128)(2,1)} async-done(((bf16[8,1,64,512]{3,2,1,0:T(8,128)(2,1)}), bf16[8,1,128,512]{3,2,1,0:T(8,128)(2,1)}) %all-gather.7.cloned.1.call-update) | async-done | bytes 1048592 | tf_op jit(solution)/shard_map/all_gather | solution.py:95
  55.5 1.7 %copy.18 = bf16[8,1,128,512]{2,0,3,1:T(8,128)(2,1)S(1)} copy(bf16[8,1,128,512]{3,2,1,0:T(8,128)(2,1)} %all-gather.7.cloned.1.call-done) | data formatting | bytes 2097152 | tf_op jit(solution)/shard_map/all_gather | solution.py:95
  57.2 0.0 copy-start.4
  57.2 1.3 %reshape.149 = bf16[1024,8,64]{0,2,1:T(8,128)(2,1)} reshape(bf16[8,1,128,512]{2,0,3,1:T(8,128)(2,1)S(1)} %copy.18) | data formatting | bytes 2097152 | tf_op jit(solution)/shard_map/while/body/eval_jaxpr/reshape | solution.py:31
  58.5 1.6 %mul.90 = f32[4,128,1024]{2,1,0:T(8,128)} broadcast(f32[4,1024]{1,0:T(4,128)S(1)} %fusion.19), dimensions={0,2} | broadcast | bytes 2113536 | tf_op jit(solution)/shard_map/while/body/eval_jaxpr/mul | solution.py:47
  60.1 0.0 copy-done.4
  60.1 10.2 %fusion.28 = (f32[512]{0:T(512)S(1)}, f32[8,512,64]{1,2,0:T(8,128)S(1)}) fusion(bf16[1024,8,64]{0,2,1:T(8,128)(2,1)} %reshape.149, bf16[512,8,64]{0,2,1:T(8,128)(2,1)S(1)} %bitcast.76, bf16[1024,8,64]{0,2,1:T(8,128)(2,1)} %reshape.148, f32[512,1024]{1,0:T(8,128)} %bitcast.73), kind=kOutput, calls=%fused_computation.47 | convolution fusion | flops 1103363584 | bytes 5769216 | tf_op jit(solution)/shard_map/while/body/eval_jaxpr/hqk,khd->qhd/dot_general | solution.py:51
  70.3 0.0 copy-start.5
  70.3 0.2 fusion.9
  70.5 1.3 %copy.19 = f32[512,512]{1,0:T(8,128)} copy(f32[512,512]{0,1:T(8,128)S(1)} %bitcast.72) | data formatting | bytes 2097152 | tf_op jit(solution)/shard_map/reshape | solution.py:100
  71.8 0.0 copy-done.5
  71.8 2.7 %fusion.5 = bf16[1,512,512]{2,1,0:T(8,128)(2,1)} fusion(bf16[512,512]{1,0:T(8,128)(2,1)S(1)} %copy-done.5, bf16[1,512,512]{2,1,0:T(8,128)(2,1)S(1)} %copy-done.1, f32[512,512]{1,0:T(8,128)} %copy.19, bf16[512,1024]{1,0:T(8,128)(2,1)} %copy-done.3, f32[512]{0:T(512)S(1)} %add_rsqrt_fusion, f32[512]{0:T(512)S(1)} %broadcast_multiply_fusion), kind=kOutput, calls=%fused_computation.10 | convolution fusion | flops 270532608 | bytes 3149824 | tf_op jit(solution)/shard_map/dot_general | solution.py:102
  (8 shorter events, 0.1 us)
Async XLA Ops:
  6.5 40.7 %copy-start = (bf16[512,1024]{1,0:T(8,128)(2,1)S(1)}, bf16[512,1024]{1,0:T(8,128)(2,1)}, u32[]{:S(2)}) copy-start(bf16[512,1024]{1,0:T(8,128)(2,1)} %param.12) | copy-start | bytes 3145732
  6.5 25.8 %copy-start.1 = (bf16[1,512,512]{2,1,0:T(8,128)(2,1)S(1)}, bf16[1,512,512]{2,1,0:T(8,128)(2,1)}, u32[]{:S(2)}) copy-start(bf16[1,512,512]{2,1,0:T(8,128)(2,1)} %param.7) | copy-start | bytes 1572868
  6.5 43.8 %all-gather.5.cloned.1.call-start = ((), (), s32[]{:S(2)}) async-start(), calls=%async_computation.2 | async-start | bytes 1572864 | tf_op jit(solution)/shard_map/all_gather | solution.py:94
  28.6 17.8 %all-to-all-start.1 = ((bf16[8,1,64,512]{3,2,1,0:T(8,128)(2,1)}), bf16[8,1,64,512]{3,2,1,0:T(8,128)(2,1)S(1)}, u32[]{:S(2)}, u32[]{:S(2)}) async-start(bf16[8,1,64,512]{3,2,1,0:T(8,128)(2,1)} %bitcast.75), calls=%async_computation.1 | async-start | bytes 1048576 | tf_op jit(solution)/shard_map/all_to_all | solution.py:76
  32.2 23.2 %all-gather.7.cloned.1.call-start = ((), (), s32[]{:S(2)}) async-start(), calls=%async_computation.3 | async-start | bytes 1572864 | tf_op jit(solution)/shard_map/all_gather | solution.py:95
  46.4 0.8 copy-start.2
  48.3 2.0 %copy-start.3 = (bf16[512,1024]{1,0:T(8,128)(2,1)}, bf16[512,1024]{1,0:T(8,128)(2,1)S(1)}, u32[]{:S(2)}) copy-start(bf16[512,1024]{1,0:T(8,128)(2,1)S(1)} %multiply_convert_fusion.1) | copy-start | bytes 3145732
  48.3 1.9 %copy-start.6 = (s32[1,8,8]{2,1,0:T(8,128)S(1)}, s32[1,8,8]{2,1,0:T(8,128)}, u32[]{:S(2)}) copy-start(s32[1,8,8]{2,1,0:T(8,128)} %param.10) | copy-start | bytes 772
  57.2 2.9 %copy-start.4 = (bf16[512,512]{0,1:T(8,128)(2,1)S(1)}, bf16[512,512]{0,1:T(8,128)(2,1)}, u32[]{:S(2)}) copy-start(bf16[512,512]{0,1:T(8,128)(2,1)} %copy.16) | copy-start | bytes 1572868
  70.3 1.5 %copy-start.5 = (bf16[512,512]{1,0:T(8,128)(2,1)S(1)}, bf16[512,512]{1,0:T(8,128)(2,1)}, u32[]{:S(2)}) copy-start(bf16[512,512]{1,0:T(8,128)(2,1)} %param.13) | copy-start | bytes 1572868
Sparse Core Ops, SparseCore 0:
  28.8 8.0 all-gather.4
  47.4 8.0 all-gather.6
where the time goes:
time: 81.7 us; the launch traced here: 81.3 us
  blocking collectives  22.1 us (27%)
  waiting for transfers between devices  15.8 us (19%)
  between operations  14.2 us (17%)
  matrix products  14 us (17%)
  local copies, waits for them, and re-layouts  10.8 us (13%)
  starting transfers between devices  3.64 us (4%)
    all_to_all x1, blocking collectives, on_device(): lax.all_to_all(hist_keys[:, None], 'hist', split_axis=0, concat_axis=1, t...  22.1 us
    all_to_all x1, waiting for transfers between devices, on_device(): lax.all_to_all(hist_values[:, None], 'hist', split_axis=0, concat_axis=1,...  13.6 us
    dot_general x1, matrix products, add_slab(): jnp.einsum('hqk,khd->qhd', weights, value_slab, preferred_element_type=jn...  10.2 us
    all_to_all x1, starting transfers between devices, on_device(): lax.all_to_all(hist_values[:, None], 'hist', split_axis=0, concat_axis=1,...  3.61 us
    dot_general x1, matrix products, on_device(): jnp.dot(mixed, out_weight, preferred_element_type=jnp.float32)  2.66 us
    all_gather x1, waiting for transfers between devices, on_device(): lax.all_gather(value_rows, 'cand', axis=1, tiled=True)  2.16 us
    all_gather x1, local copies, waits for them, and re-layouts, on_device(): lax.all_gather(key_rows, 'cand', axis=1, tiled=True)  1.72 us
    all_gather x1, local copies, waits for them, and re-layouts, on_device(): lax.all_gather(value_rows, 'cand', axis=1, tiled=True)  1.71 us
  transfers between devices with their start and end apart: 3, of which 2 were waited for; matrix products, arithmetic and copies ran while one was open for 7% of the time, Pallas kernels for 0%

commit v1 on v0

--- a/solution.py
+++ b/solution.py
@@ -72,7 +72,15 @@
     live_blocks = (jnp.arange(block_total, dtype=jnp.int32) < hist_blocks[0]).astype(jnp.float32)
     mask_eff = block_mask[0].astype(jnp.float32) * live_blocks[None, :]
     arrived_keys, arrived_values = (
-        lax.all_to_all(hist_keys[:, None], "hist", split_axis=0, concat_axis=1, tiled=True),
+        jnp.concatenate(
+            lax.all_to_all(
+                jnp.stack(jnp.split(hist_keys[:, None], lax.axis_size("hist"), axis=0)),
+                "hist",
+                0,
+                0,
+            ),
+            axis=1,
+        ),
         lax.all_to_all(hist_values[:, None], "hist", split_axis=0, concat_axis=1, tiled=True),
     )
     key_rows = arrived_keys[0]

time: 81.7 us -> 84.8 us (1.038)
  blocking collectives: 22.1 us -> 0 us
  local copies, waits for them, and re-layouts: 10.8 us -> 23.2 us
  starting transfers between devices: 3.64 us -> 11.1 us
  waiting for transfers between devices: 15.8 us -> 20.6 us
    all_to_all x1 -> x0, blocking collectives: 22.1 us -> none  [on_device(): lax.all_to_all(hist_keys[:, None], 'hist', split_axis=0, concat_axis=1, t...]
    all_to_all x0 -> x1, waiting for transfers between devices: none -> 14.1 us  [on_device(): lax.all_to_all(jnp.stack(jnp.split(hist_keys[:, None], lax.axis_size('his...]
    unnamed x14 -> x23, local copies, waits for them, and re-layouts: 0.82 us -> 11.8 us
    all_to_all x1, waiting for transfers between devices: 13.6 us -> 4.22 us  [on_device(): lax.all_to_all(hist_values[:, None], 'hist', split_axis=0, concat_axis=1,...]
    all_to_all x1, starting transfers between devices: 3.61 us -> 7.44 us  [on_device(): lax.all_to_all(hist_values[:, None], 'hist', split_axis=0, concat_axis=1,...]
    all_to_all x0 -> x1, starting transfers between devices: none -> 3.64 us  [on_device(): lax.all_to_all(jnp.stack(jnp.split(hist_keys[:, None], lax.axis_size('his...]
    all_gather x1, waiting for transfers between devices: 0.01 us -> 2.17 us  [on_device(): lax.all_gather(key_rows, 'cand', axis=1, tiled=True)]
    all_gather x1, waiting for transfers between devices: 2.16 us -> 0.01 us  [on_device(): lax.all_gather(value_rows, 'cand', axis=1, tiled=True)]
  transfers between devices with their start and end apart: 3 -> 4, of which waited for: 2 -> 3; matrix products, arithmetic and copies ran while one was open for 7% -> 21% of each run, Pallas kernels for 0% -> 0%
where the time goes in v1:
time: 84.8 us; the launch traced here: 84 us
  local copies, waits for them, and re-layouts  23.2 us (27%)
  waiting for transfers between devices  20.6 us (24%)
  between operations  14.3 us (17%)
  matrix products  14 us (17%)
  starting transfers between devices  11.1 us (13%)
    all_to_all x1, waiting for transfers between devices, on_device(): lax.all_to_all(jnp.stack(jnp.split(hist_keys[:, None], lax.axis_size('his...  14.1 us
    unnamed x23, local copies, waits for them, and re-layouts  11.8 us
    dot_general x1, matrix products, add_slab(): jnp.einsum('hqk,khd->qhd', weights, value_slab, preferred_element_type=jn...  10.2 us
    all_to_all x1, starting transfers between devices, on_device(): lax.all_to_all(hist_values[:, None], 'hist', split_axis=0, concat_axis=1,...  7.44 us
    all_to_all x1, waiting for transfers between devices, on_device(): lax.all_to_all(hist_values[:, None], 'hist', split_axis=0, concat_axis=1,...  4.22 us
    all_to_all x1, starting transfers between devices, on_device(): lax.all_to_all(jnp.stack(jnp.split(hist_keys[:, None], lax.axis_size('his...  3.64 us
    dot_general x1, matrix products, on_device(): jnp.dot(mixed, out_weight, preferred_element_type=jnp.float32)  2.66 us
    all_gather x1, waiting for transfers between devices, on_device(): lax.all_gather(key_rows, 'cand', axis=1, tiled=True)  2.17 us
  transfers between devices with their start and end apart: 4, of which 3 were waited for; matrix products, arithmetic and copies ran while one was open for 21% of the time, Pallas kernels for 0%

profile of v1, /device:TPU:0, one launch (start us, length us, event | category | flops | bytes accessed | tf_op | source)
XLA Modules:
  0.0 84.0 jit_solution(5717797832430615762)
XLA Ops:
  6.5 0.0 copy-start
  6.5 0.0 copy-start.1
  6.5 7.4 %all-to-all-start.1 = ((bf16[8,1,64,512]{3,2,1,0:T(8,128)(2,1)}), bf16[8,1,64,512]{3,2,1,0:T(8,128)(2,1)S(1)}, u32[]{:S(2)}, u32[]{:S(2)}) async-start(bf16[8,1,64,512]{3,2,1,0:T(8,128)(2,1)} %bitcast.89), calls=%async_computation.1 | async-start | bytes 1048576 | tf_op jit(solution)/shard_map/all_to_all | solution.py:84
  14.0 0.0 all-gather.7.cloned.1.call-start
  14.0 1.5 %bitcast_dynamic-update-slice_fusion.7 = bf16[8,1,1,64,512]{4,3,2,1,0:T(8,128)(2,1)} fusion(bf16[8,64,512]{2,1,0:T(8,128)(2,1)} %param.8), kind=kLoop, calls=%fused_computation.30 | loop fusion | bytes 131072
  15.5 1.5 %bitcast_dynamic-update-slice_fusion.6 = bf16[8,1,1,64,512]{4,3,2,1,0:T(8,128)(2,1)} fusion(bf16[8,1,1,64,512]{4,3,2,1,0:T(8,128)(2,1)} %bitcast_dynamic-update-slice_fusion.7, bf16[8,64,512]{2,1,0:T(8,128)(2,1)} %param.8), kind=kLoop, calls=%fused_computation.29 | loop fusion | bytes 131072
  16.9 1.5 %bitcast_dynamic-update-slice_fusion.5 = bf16[8,1,1,64,512]{4,3,2,1,0:T(8,128)(2,1)} fusion(bf16[8,1,1,64,512]{4,3,2,1,0:T(8,128)(2,1)} %bitcast_dynamic-update-slice_fusion.6, bf16[8,64,512]{2,1,0:T(8,128)(2,1)} %param.8), kind=kLoop, calls=%fused_computation.28 | loop fusion | bytes 131072
  18.4 1.5 %bitcast_dynamic-update-slice_fusion.4 = bf16[8,1,1,64,512]{4,3,2,1,0:T(8,128)(2,1)} fusion(bf16[8,1,1,64,512]{4,3,2,1,0:T(8,128)(2,1)} %bitcast_dynamic-update-slice_fusion.5, bf16[8,64,512]{2,1,0:T(8,128)(2,1)} %param.8), kind=kLoop, calls=%fused_computation.27 | loop fusion | bytes 131072
  19.9 1.5 %bitcast_dynamic-update-slice_fusion.3 = bf16[8,1,1,64,512]{4,3,2,1,0:T(8,128)(2,1)} fusion(bf16[8,1,1,64,512]{4,3,2,1,0:T(8,128)(2,1)} %bitcast_dynamic-update-slice_fusion.4, bf16[8,64,512]{2,1,0:T(8,128)(2,1)} %param.8), kind=kLoop, calls=%fused_computation.26 | loop fusion | bytes 131072
  21.3 1.5 %bitcast_dynamic-update-slice_fusion.2 = bf16[8,1,1,64,512]{4,3,2,1,0:T(8,128)(2,1)} fusion(bf16[8,1,1,64,512]{4,3,2,1,0:T(8,128)(2,1)} %bitcast_dynamic-update-slice_fusion.3, bf16[8,64,512]{2,1,0:T(8,128)(2,1)} %param.8), kind=kLoop, calls=%fused_computation.25 | loop fusion | bytes 131072
  22.8 1.5 %bitcast_dynamic-update-slice_fusion.1 = bf16[8,1,1,64,512]{4,3,2,1,0:T(8,128)(2,1)} fusion(bf16[8,1,1,64,512]{4,3,2,1,0:T(8,128)(2,1)} %bitcast_dynamic-update-slice_fusion.2, bf16[8,64,512]{2,1,0:T(8,128)(2,1)} %param.8), kind=kLoop, calls=%fused_computation.24 | loop fusion | bytes 131072
  24.2 4.2 %all-to-all-done.1 = bf16[8,1,64,512]{3,2,1,0:T(8,128)(2,1)S(1)} async-done(((bf16[8,1,64,512]{3,2,1,0:T(8,128)(2,1)}), bf16[8,1,64,512]{3,2,1,0:T(8,128)(2,1)S(1)}, u32[]{:S(2)}, u32[]{:S(2)}) %all-to-all-start.1) | async-done | bytes 524320 | tf_op jit(solution)/shard_map/all_to_all | solution.py:84
  28.5 0.0 copy-start.2
  28.5 0.8 copy-done.2
  29.3 0.0 all-gather.7.cloned.1.call-update
  29.3 1.5 %bitcast_dynamic-update-slice_fusion = bf16[8,1,1,64,512]{4,3,2,1,0:T(8,128)(2,1)} fusion(bf16[8,1,1,64,512]{4,3,2,1,0:T(8,128)(2,1)} %bitcast_dynamic-update-slice_fusion.1, bf16[8,64,512]{2,1,0:T(8,128)(2,1)} %param.8), kind=kLoop, calls=%fused_computation.23 | loop fusion | bytes 131072 | tf_op jit(solution)/shard_map/stack | solution.py:77
  30.8 3.6 %all-to-all-start = ((bf16[8,1,1,64,512]{4,3,2,1,0:T(8,128)(2,1)}), bf16[8,1,1,64,512]{4,3,2,1,0:T(8,128)(2,1)S(1)}, u32[]{:S(2)}, u32[]{:S(2)}) async-start(bf16[8,1,1,64,512]{4,3,2,1,0:T(8,128)(2,1)} %bitcast_dynamic-update-slice_fusion), calls=%async_computation | async-start | bytes 1048576 | tf_op jit(solution)/shard_map/all_to_all | solution.py:76
  34.4 0.0 all-gather.5.cloned.1.call-start
  34.4 0.0 copy-done.1
  34.4 0.1 convert_reduce_fusion
  34.6 0.3 fusion.6
  34.9 14.1 %all-to-all-done = bf16[8,1,1,64,512]{4,3,2,1,0:T(8,128)(2,1)S(1)} async-done(((bf16[8,1,1,64,512]{4,3,2,1,0:T(8,128)(2,1)}), bf16[8,1,1,64,512]{4,3,2,1,0:T(8,128)(2,1)S(1)}, u32[]{:S(2)}, u32[]{:S(2)}) %all-to-all-start) | async-done | bytes 524320 | tf_op jit(solution)/shard_map/all_to_all | solution.py:76
  49.1 0.0 copy-start.3
  49.1 0.8 copy-done.3
  49.9 0.0 all-gather.5.cloned.1.call-update
  49.9 0.0 copy-done
  49.9 1.0 %multiply_convert_fusion.1 = bf16[512,1024]{1,0:T(8,128)(2,1)S(1)} fusion(bf16[512,1024]{1,0:T(8,128)(2,1)S(1)} %copy-done, bf16[1,512,512]{2,1,0:T(8,128)(2,1)S(1)} %copy-done.1, f32[512]{0:T(512)S(1)} %add_rsqrt_fusion.1, f32[512]{0:T(512)S(1)} %broadcast_multiply_fusion.1), kind=kOutput, calls=%fused_computation.1 | convolution fusion | flops 540540928 | bytes 2625536 | tf_op jit(solution)/shard_map/dot_general | solution.py:66
  50.9 0.0 copy-start.4
  50.9 0.0 copy-start.7
  51.7 1.0 %copy.16 = bf16[512,512]{0,1:T(8,128)(2,1)} copy(bf16[512,512]{1,0:T(8,128)(2,1)S(1)} %slice.16) | data formatting | bytes 1048576 | tf_op jit(solution)/shard_map/slice | solution.py:69
  52.7 0.1 add_select_fusion
  52.8 0.0 copy-done.7
  52.8 0.1 fusion.19
  52.9 0.0 copy-done.4
  53.0 1.7 %copy.18 = bf16[8,1,128,512]{2,0,3,1:T(8,128)(2,1)S(1)} copy(bf16[8,1,128,512]{3,2,1,0:T(8,128)(2,1)} %all-gather.7.cloned.1.call-done) | data formatting | bytes 2097152 | tf_op jit(solution)/shard_map/all_gather | solution.py:103
  54.7 1.3 %reshape.161 = bf16[1024,8,64]{0,2,1:T(8,128)(2,1)} reshape(bf16[8,1,128,512]{2,0,3,1:T(8,128)(2,1)S(1)} %copy.18) | data formatting | bytes 2097152 | tf_op jit(solution)/shard_map/while/body/eval_jaxpr/reshape | solution.py:31
  55.9 2.2 %all-gather.5.cloned.1.call-done = bf16[8,1,1,128,512]{4,3,2,1,0:T(8,128)(2,1)} async-done(((bf16[8,1,1,64,512]{4,3,2,1,0:T(8,128)(2,1)}), bf16[8,1,1,128,512]{4,3,2,1,0:T(8,128)(2,1)}) %all-gather.5.cloned.1.call-update) | async-done | bytes 1048592 | tf_op jit(solution)/shard_map/all_gather | solution.py:102
  58.1 1.7 %copy.17 = bf16[8,1,1,128,512]{3,0,4,2,1:T(8,128)(2,1)S(1)} copy(bf16[8,1,1,128,512]{4,3,2,1,0:T(8,128)(2,1)} %all-gather.5.cloned.1.call-done) | data formatting | bytes 2097152 | tf_op jit(solution)/shard_map/all_gather | solution.py:102
  59.8 0.0 copy-start.5
  59.8 1.3 %reshape.160 = bf16[1024,8,64]{0,2,1:T(8,128)(2,1)} reshape(bf16[8,1,1,128,512]{3,0,4,2,1:T(8,128)(2,1)S(1)} %copy.17) | data formatting | bytes 2097152 | tf_op jit(solution)/shard_map/while/body/eval_jaxpr/reshape | solution.py:30
  61.1 1.6 %mul.90 = f32[4,128,1024]{2,1,0:T(8,128)} broadcast(f32[4,1024]{1,0:T(4,128)S(1)} %fusion.19), dimensions={0,2} | broadcast | bytes 2113536 | tf_op jit(solution)/shard_map/while/body/eval_jaxpr/mul | solution.py:47
  62.7 0.0 copy-done.5
  62.7 10.2 %fusion.28 = (f32[512]{0:T(512)S(1)}, f32[8,512,64]{1,2,0:T(8,128)S(1)}) fusion(bf16[1024,8,64]{0,2,1:T(8,128)(2,1)} %reshape.161, bf16[512,8,64]{0,2,1:T(8,128)(2,1)S(1)} %bitcast.90, bf16[1024,8,64]{0,2,1:T(8,128)(2,1)} %reshape.160, f32[512,1024]{1,0:T(8,128)} %bitcast.88), kind=kOutput, calls=%fused_computation.55 | convolution fusion | flops 1103363584 | bytes 5769216 | tf_op jit(solution)/shard_map/while/body/eval_jaxpr/hqk,khd->qhd/dot_general | solution.py:51
  73.0 0.0 copy-start.6
  73.0 0.2 fusion.9
  73.2 1.3 %copy.19 = f32[512,512]{1,0:T(8,128)} copy(f32[512,512]{0,1:T(8,128)S(1)} %bitcast.87) | data formatting | bytes 2097152 | tf_op jit(solution)/shard_map/reshape | solution.py:108
  74.5 0.0 copy-done.6
  74.5 2.7 %fusion.5 = bf16[1,512,512]{2,1,0:T(8,128)(2,1)} fusion(bf16[512,512]{1,0:T(8,128)(2,1)S(1)} %copy-done.6, bf16[1,512,512]{2,1,0:T(8,128)(2,1)S(1)} %copy-done.1, f32[512,512]{1,0:T(8,128)} %copy.19, bf16[512,1024]{1,0:T(8,128)(2,1)} %copy-done.4, f32[512]{0:T(512)S(1)} %add_rsqrt_fusion, f32[512]{0:T(512)S(1)} %broadcast_multiply_fusion), kind=kOutput, calls=%fused_computation.10 | convolution fusion | flops 270532608 | bytes 3149824 | tf_op jit(solution)/shard_map/dot_general | solution.py:110
  (9 shorter events, 0.1 us)
Async XLA Ops:
  6.5 43.4 %copy-start = (bf16[512,1024]{1,0:T(8,128)(2,1)S(1)}, bf16[512,1024]{1,0:T(8,128)(2,1)}, u32[]{:S(2)}) copy-start(bf16[512,1024]{1,0:T(8,128)(2,1)} %param.12) | copy-start | bytes 3145732
  6.5 27.9 %copy-start.1 = (bf16[1,512,512]{2,1,0:T(8,128)(2,1)S(1)}, bf16[1,512,512]{2,1,0:T(8,128)(2,1)}, u32[]{:S(2)}) copy-start(bf16[1,512,512]{2,1,0:T(8,128)(2,1)} %param.7) | copy-start | bytes 1572868
  6.5 21.9 %all-to-all-start.1 = ((bf16[8,1,64,512]{3,2,1,0:T(8,128)(2,1)}), bf16[8,1,64,512]{3,2,1,0:T(8,128)(2,1)S(1)}, u32[]{:S(2)}, u32[]{:S(2)}) async-start(bf16[8,1,64,512]{3,2,1,0:T(8,128)(2,1)} %bitcast.89), calls=%async_computation.1 | async-start | bytes 1048576 | tf_op jit(solution)/shard_map/all_to_all | solution.py:84
  14.0 39.0 %all-gather.7.cloned.1.call-start = ((), (), s32[]{:S(2)}) async-start(), calls=%async_computation.3 | async-start | bytes 1572864 | tf_op jit(solution)/shard_map/all_gather | solution.py:103
  28.5 0.8 copy-start.2
  30.8 18.3 %all-to-all-start = ((bf16[8,1,1,64,512]{4,3,2,1,0:T(8,128)(2,1)}), bf16[8,1,1,64,512]{4,3,2,1,0:T(8,128)(2,1)S(1)}, u32[]{:S(2)}, u32[]{:S(2)}) async-start(bf16[8,1,1,64,512]{4,3,2,1,0:T(8,128)(2,1)} %bitcast_dynamic-update-slice_fusion), calls=%async_computation | async-start | bytes 1048576 | tf_op jit(solution)/shard_map/all_to_all | solution.py:76
  34.4 23.7 %all-gather.5.cloned.1.call-start = ((), (), s32[]{:S(2)}) async-start(), calls=%async_computation.2 | async-start | bytes 1572864 | tf_op jit(solution)/shard_map/all_gather | solution.py:102
  49.1 0.8 copy-start.3
  50.9 2.0 %copy-start.4 = (bf16[512,1024]{1,0:T(8,128)(2,1)}, bf16[512,1024]{1,0:T(8,128)(2,1)S(1)}, u32[]{:S(2)}) copy-start(bf16[512,1024]{1,0:T(8,128)(2,1)S(1)} %multiply_convert_fusion.1) | copy-start | bytes 3145732
  50.9 1.9 %copy-start.7 = (s32[1,8,8]{2,1,0:T(8,128)S(1)}, s32[1,8,8]{2,1,0:T(8,128)}, u32[]{:S(2)}) copy-start(s32[1,8,8]{2,1,0:T(8,128)} %param.10) | copy-start | bytes 772
  59.8 2.9 %copy-start.5 = (bf16[512,512]{0,1:T(8,128)(2,1)S(1)}, bf16[512,512]{0,1:T(8,128)(2,1)}, u32[]{:S(2)}) copy-start(bf16[512,512]{0,1:T(8,128)(2,1)} %copy.16) | copy-start | bytes 1572868
  73.0 1.5 %copy-start.6 = (bf16[512,512]{1,0:T(8,128)(2,1)S(1)}, bf16[512,512]{1,0:T(8,128)(2,1)}, u32[]{:S(2)}) copy-start(bf16[512,512]{1,0:T(8,128)(2,1)} %param.13) | copy-start | bytes 1572868
Sparse Core Ops, SparseCore 0:
  29.4 8.0 all-gather.6
  50.0 8.0 all-gather.4
